TPU v7x, 32 devices: a whole 2x2x4 slice. The times are simulated.
32 devices in a mesh: gx: 8 (over z, y), gy: 2 (over x), gz: 2 (over core).
Axes of the slice: x: 2, y: 2, z: 4, core: 2. Of those that a mesh axis runs over, the one named last changes fastest.
Arguments:
- tensor_blocks: bfloat16 [8, 2, 2, 2, 128, 128, 128], P('gx', 'gy', 'gz'), may hold values from -768 to 768
- block_coords: int32 [8, 2, 2, 2, 3], P('gx', 'gy', 'gz'), may hold values from 0 to 1, as said below
- live_counts: int32 [8, 2, 2], P('gx', 'gy', 'gz'), may hold values from 1 to 2, as said below
- factor_a: bfloat16 [8, 256, 256], P('gx', ('gy', 'gz')), may hold values from 0.049804688 to 1
- factor_b: bfloat16 [2, 256, 256], P('gy', ('gx', 'gz')), may hold values from 0.049804688 to 1
- factor_c: bfloat16 [2, 256, 256], P('gz', ('gx', 'gy')), may hold values from 0.049804688 to 1
Outputs:
- updated_a: bfloat16 [8, 256, 256], P('gx', ('gy', 'gz'))
- updated_b: bfloat16 [2, 256, 256], P('gy', ('gx', 'gz'))
- updated_c: bfloat16 [2, 256, 256], P('gz', ('gx', 'gy'))
Inputs may be any that keep to these rules, and one draw needn't show every extreme that they name: `block_coords`: within one cell the 2 slots hold distinct positions. `live_counts`: some cell has exactly 2 live slots and another exactly one.
All inputs are finite; a program needn't handle non-finite values. Where the computation divides by a largest or mean magnitude, that divisor is 1e-20 or more.
Results may differ from a plain program's by a relative error of at most 0.0055.
Values may be sent and summed in bfloat16 or wider, within the bound.
No kernel may reach another device: no remote copies, remote signals or barrier semaphores. Data moves between devices by JAX's collectives and lax.ppermute only.
A program may use at most 256 MiB of HBM per device.

v0:
```python
import jax
import jax.numpy as jnp
from jax import lax
from jax.sharding import PartitionSpec as P

NS_STEPS = 8
ADMM_ITERS = 4
HIGHEST = lax.Precision.HIGHEST


def gram_rows(factor):
    return lax.dot_general(
        factor, factor, (((0,), (0,)), ((), ())), preferred_element_type=jnp.float32
    )


def newton_inverse(gram_left, gram_right):
    weighted = gram_left * gram_right
    width = weighted.shape[0]
    identity = jnp.eye(width, dtype=weighted.dtype)
    penalty = jnp.trace(weighted) / width
    system = weighted + penalty * identity
    bound = jnp.max(jnp.sum(jnp.abs(system), axis=1))
    inverse = identity / bound
    for step in range(NS_STEPS):
        inverse = jnp.dot(
            inverse, 2.0 * identity - jnp.dot(system, inverse, precision=HIGHEST), precision=HIGHEST
        )
    return (penalty, inverse)


def split_updates(totals, start, penalty, inverse):
    primal = start.astype(jnp.float32)
    dual = jnp.zeros_like(primal)
    for step in range(ADMM_ITERS):
        target = jnp.dot(totals + penalty * (primal + dual), inverse, precision=HIGHEST)
        primal = jnp.maximum(target - dual, 0.0)
        dual = dual + primal - target
    return primal.astype(jnp.bfloat16)


def on_device(tensor_blocks, block_coords, live_counts, factor_a, factor_b, factor_c):
    slot_count = tensor_blocks.shape[3]
    side = tensor_blocks.shape[4]
    width = factor_a.shape[2]
    blocks = tensor_blocks.reshape(slot_count, side, side, side)
    triples = block_coords.reshape(slot_count, 3)
    live_total = live_counts.reshape(())
    own_a = factor_a[0]
    own_b = factor_b[0]
    own_c = factor_c[0]
    slab_b = lax.all_gather(own_b, ("gx", "gz"), axis=0, tiled=True)
    slab_c = lax.all_gather(own_c, ("gx", "gy"), axis=0, tiled=True)
    height = slab_b.shape[0]
    gram_b = lax.psum(gram_rows(slab_b), "gy")
    gram_c = lax.psum(gram_rows(slab_c), "gz")

    def fetch(position):
        block = lax.dynamic_index_in_dim(blocks, position, 0, keepdims=False)
        triple = lax.dynamic_index_in_dim(triples, position, 0, keepdims=False)
        return (block, triple * side)

    def accumulate(running, row_start, terms):
        current = lax.dynamic_slice_in_dim(running, row_start, side, 0)
        return lax.dynamic_update_slice_in_dim(running, current + terms, row_start, 0)

    def first_visit(position, running):
        block, starts = fetch(position)
        band_b = lax.dynamic_slice_in_dim(slab_b, starts[1], side, 0)
        band_c = lax.dynamic_slice_in_dim(slab_c, starts[2], side, 0)
        contracted = jnp.dot(
            block.reshape(side * side, side), band_c, preferred_element_type=jnp.float32
        ).reshape(side, side, width)
        terms = jnp.sum(contracted * band_b.astype(jnp.float32)[None], axis=1)
        return accumulate(running, starts[0], terms)

    empty = jnp.zeros((height, width), jnp.float32)
    partial_a = lax.fori_loop(0, live_total, first_visit, empty)
    sums_a = lax.psum_scatter(partial_a, ("gy", "gz"), scatter_dimension=0, tiled=True)
    penalty, inverse = newton_inverse(gram_b, gram_c)
    new_a = split_updates(sums_a, own_a, penalty, inverse)
    slab_a = lax.all_gather(new_a, ("gy", "gz"), axis=0, tiled=True)
    gram_a = lax.psum(gram_rows(slab_a), "gx")

    def second_visit(position, state):
        running, stored = state
        block, starts = fetch(position)
        band_a = lax.dynamic_slice_in_dim(slab_a, starts[0], side, 0)
        band_c = lax.dynamic_slice_in_dim(slab_c, starts[2], side, 0)
        projected = lax.dot_general(
            band_a,
            block.reshape(side, side * side),
            (((0,), (0,)), ((), ())),
            preferred_element_type=jnp.float32,
        )
        terms = jnp.sum(
            projected.reshape(width, side, side) * band_c.astype(jnp.float32).T[:, None, :], axis=2
        ).T
        stored = lax.dynamic_update_index_in_dim(stored, projected, position, 0)
        return (accumulate(running, starts[1], terms), stored)

    holder = jnp.zeros((slot_count, width, side * side), jnp.float32)
    partial_b, stored = lax.fori_loop(0, live_total, second_visit, (empty, holder))
    sums_b = lax.psum_scatter(partial_b, ("gx", "gz"), scatter_dimension=0, tiled=True)
    penalty, inverse = newton_inverse(gram_a, gram_c)
    new_b = split_updates(sums_b, own_b, penalty, inverse)
    slab_b_new = lax.all_gather(new_b, ("gx", "gz"), axis=0, tiled=True)
    gram_b_new = lax.psum(gram_rows(slab_b_new), "gy")

    def third_visit(position, running):
        projected = lax.dynamic_index_in_dim(stored, position, 0, keepdims=False)
        starts = lax.dynamic_index_in_dim(triples, position, 0, keepdims=False) * side
        band_b = lax.dynamic_slice_in_dim(slab_b_new, starts[1], side, 0)
        terms = jnp.sum(
            projected.reshape(width, side, side) * band_b.astype(jnp.float32).T[:, :, None], axis=1
        ).T
        return accumulate(running, starts[2], terms)

    partial_c = lax.fori_loop(0, live_total, third_visit, empty)
    sums_c = lax.psum_scatter(partial_c, ("gx", "gy"), scatter_dimension=0, tiled=True)
    penalty, inverse = newton_inverse(gram_a, gram_b_new)
    new_c = split_updates(sums_c, own_c, penalty, inverse)
    return (new_a[None], new_b[None], new_c[None])


def solution(mesh):
    return jax.shard_map(
        on_device,
        mesh=mesh,
        in_specs=(
            P("gx", "gy", "gz", None, None, None, None),
            P("gx", "gy", "gz", None, None),
            P("gx", "gy", "gz"),
            P("gx", ("gy", "gz"), None),
            P("gy", ("gx", "gz"), None),
            P("gz", ("gx", "gy"), None),
        ),
        out_specs=(
            P("gx", ("gy", "gz"), None),
            P("gy", ("gx", "gz"), None),
            P("gz", ("gx", "gy"), None),
        ),
        check_vma=False,
    )
```

profile of v0, /device:TPU:0, one launch (start us, length us, event | category | flops | bytes accessed | tf_op | source)
XLA Modules:
  0.0 451.7 jit_solution(6024621092706022354)
XLA Ops:
  8.0 43.3 %all-gather = bf16[1,256,256]{2,1,0:T(8,128)(2,1)S(1)} all-gather(bf16[1,16,256]{2,1,0:T(8,128)(2,1)} %param.17), channel_id=2, replica_groups=mesh['gx'=8,'gy'=2,'gz'=2] {'gx','gy'}, dimensions={1}, use_global_device_ids=true | all-gather | bytes 139264 | tf_op jit(solution)/shard_map/all_gather | solution.py:53
  52.4 17.8 %all-gather.1 = bf16[1,256,256]{2,1,0:T(8,128)(2,1)S(1)} all-gather(bf16[1,16,256]{2,1,0:T(8,128)(2,1)} %param.16), channel_id=3, replica_groups=mesh['gx'=8,'gy'=2,'gz'=2] {'gx','gz'}, dimensions={1}, use_global_device_ids=true | all-gather | bytes 139264 | tf_op jit(solution)/shard_map/all_gather | solution.py:52
  71.2 14.1 %while.32 = (s32[]{:T(128)}, f32[256,256]{1,0:T(8,128)S(1)}, s32[]{:T(128)}, s32[2,3]{1,0:T(2,128)}, bf16[2,128,128,128]{3,2,1,0:T(8,128)(2,1)}, /*index=5*/bf16...) while((s32[]{:T(128)}, f32[256,256]{1,0:T(8,128)S(1)}, ...), condition=%wide.region_2.3_spmd, body=%wide.region_0.2_spmd.sunk | while | flops 1082163200 | bytes 5374269 | solution.py:78
  77.1 4.5 %multiply_reduce_fusion.4 = f32[128,256]{1,0:T(8,128)S(1)} fusion(f32[128,256]{1,0:T(8,128)S(1)} %dynamic-slice_convert_fusion.2, bf16[2,128,128,128]{3,2,1,0:T(8,128)(2,1)} %get-tuple-element.385, s32[]{:T(128)S(6)} %select_n.72, bf16[256,256]{1,0:T(8,128)(2,1)S(1)} %get-tuple-element.386, s32[]{:T(128)S(6)} %select_n.74), kind=kOutput, calls=%fused_computation.clone.1 | convolution fusion | flops 1082097664 | bytes 4521992 | tf_op jit(solution)/shard_map/while/body/dot_general | solution.py:71
  86.1 7.3 %all-reduce.5.cloned.1.call-done = f32[256,256]{1,0:T(8,128)} async-done(((f32[256,256]{1,0:T(8,128)}), f32[256,256]{1,0:T(8,128)}) %all-reduce.5.cloned.1.call-update) | async-done | bytes 262160 | tf_op jit(solution)/shard_map/psum | solution.py:55
  93.4 1.7 select_reduce_fusion.2
  103.5 13.3 %reduce-scatter.4.cloned.1.call-done = f32[64,256]{1,0:T(8,128)} async-done(((f32[256,256]{1,0:T(8,128)}), f32[64,256]{1,0:T(8,128)}) %reduce-scatter.4.cloned.1.call-update) | async-done | bytes 65552 | tf_op jit(solution)/shard_map/reduce_scatter | solution.py:79
  121.2 5.4 %all_gather.14 = bf16[256,256]{1,0:T(8,128)(2,1)S(1)} all-gather(bf16[64,256]{1,0:T(8,128)(2,1)S(1)} %fusion.15), channel_id=1, replica_groups=mesh['gx'=8,'gy'=2,'gz'=2] {'gy','gz'}, dimensions={0}, use_global_device_ids=true | all-gather | bytes 163840 | tf_op jit(solution)/shard_map/all_gather | solution.py:82
  127.6 11.0 %broadcast_in_dim.28 = f32[2,256,16384]{2,1,0:T(8,128)} broadcast(f32[]{:T(128)} %constant.86.clone.1), dimensions={} | broadcast | bytes 33554436 | tf_op jit(solution)/shard_map/broadcast_in_dim | solution.py:102
  138.7 49.5 %while.33 = (s32[]{:T(128)}, f32[256,256]{1,0:T(8,128)S(1)}, f32[2,256,16384]{2,1,0:T(8,128)}, s32[]{:T(128)}, s32[2,3]{1,0:T(2,128)S(1)}, /*index=5*/bf16[256,2...) while((s32[]{:T(128)}, f32[256,256]{1,0:T(8,128)S(1)}, ...), condition=%wide.region_11.12_spmd, body=%wide.region_9.11_spmd.sunk | while | flops 1082163200 | bytes 98697544 | solution.py:103
  142.3 2.5 constant_dynamic-slice_fusion.14
  144.8 15.0 %bitcast_dynamic-update-slice_fusion.2 = (f32[2,256,16384]{2,1,0:T(8,128)}, f32[256,16384]{1,0:T(8,128)}) fusion(f32[2,256,16384]{2,1,0:T(8,128)} %get-tuple-element.406, s32[]{:T(128)S(6)} %select_n.76, bf16[16,8,128,128]{3,2,1,0:T(8,128)(2,1)S(1)} %bitcast.188, bf16[256,256]{1,0:T(8,128)(2,1)S(1)} %get-tuple-element.421, s32[]{:T(128)S(6)} %select_n.78), kind=kOutput, calls=%fused_computation.10.clone.1 | convolution fusion | flops 1073741824 | bytes 37814280 | tf_op jit(solution)/shard_map/while/body/dot_general | solution.py:90
  159.8 14.1 %copy.52 = f32[32,8,128,128]{3,2,1,0:T(8,128)} copy(f32[32,8,128,128]{3,1,2,0:T(8,128)} %bitcast.187) | data formatting | bytes 33554432 | tf_op jit(solution)/shard_map/while
  176.0 8.2 %multiply_reduce_fusion.5 = f32[256,128]{1,0:T(8,128)S(1)} fusion(f32[256,128,128]{2,1,0:T(8,128)} %bitcast.186, f32[256,128]{1,0:T(8,128)S(1)} %convert_bitcast_fusion.4), kind=kLoop, calls=%fused_computation.11.clone.1 | loop fusion | flops 8355840 | bytes 17039360 | tf_op jit(solution)/shard_map/while/body/reduce_sum | solution.py:96
  189.2 9.5 %all-reduce.9.cloned.1.call-done = f32[256,256]{1,0:T(8,128)} async-done(((f32[256,256]{1,0:T(8,128)}), f32[256,256]{1,0:T(8,128)}) %all-reduce.9.cloned.1.call-update) | async-done | bytes 262160 | tf_op jit(solution)/shard_map/psum | solution.py:83
  198.7 1.6 select_reduce_fusion.1
  208.7 84.3 %reduce-scatter.6.cloned.1.call-done = f32[16,256]{1,0:T(8,128)} async-done(((f32[256,256]{1,0:T(8,128)}), f32[16,256]{1,0:T(8,128)}) %reduce-scatter.6.cloned.1.call-update) | async-done | bytes 16400 | tf_op jit(solution)/shard_map/reduce_scatter | solution.py:104
  296.8 19.8 %all_gather.15 = bf16[256,256]{1,0:T(8,128)(2,1)S(1)} all-gather(bf16[16,256]{1,0:T(8,128)(2,1)S(1)} %fusion.18), channel_id=1, replica_groups=mesh['gx'=8,'gy'=2,'gz'=2] {'gx','gz'}, dimensions={0}, use_global_device_ids=true | all-gather | bytes 139264 | tf_op jit(solution)/shard_map/all_gather | solution.py:107
  317.6 24.1 %while.34 = (s32[]{:T(128)}, f32[256,256]{1,0:T(8,128)S(1)}, s32[]{:T(128)}, s32[2,3]{1,0:T(2,128)S(1)}, f32[2,256,16384]{2,1,0:T(8,128)}, /*index=5*/bf16[256,2...) while((s32[]{:T(128)}, f32[256,256]{1,0:T(8,128)S(1)}, s32[]{:T(128)}, ...), condition=%wide.region_19.20_spmd, body=%wide.region_17.19_spmd.sunk | while | flops 8421390 | bytes 86049016 | solution.py:119
  321.0 6.6 %dynamic-slice_bitcast_fusion.2 = f32[32,8,128,128]{3,1,2,0:T(8,128)S(1)} fusion(f32[2,256,16384]{2,1,0:T(8,128)} %get-tuple-element.452, s32[]{:T(128)S(6)} %select_n.80), kind=kLoop, calls=%fused_computation.26.clone.1 | loop fusion | bytes 33554436 | tf_op jit(solution)/shard_map/while
  327.7 3.8 copy.56
  331.5 6.1 %fusion.282 = f32[256,128]{1,0:T(8,128)S(1)} fusion(f32[32,8,128,128]{3,2,1,0:T(8,128)S(1)} %copy.56, f32[256,128]{1,0:T(8,128)S(1)} %convert_bitcast_fusion.5), kind=kLoop, calls=%fused_computation.25.clone.1 | loop fusion | flops 8355840 | bytes 17039360 | tf_op jit(solution)/shard_map/while/body/reduce_sum | solution.py:114
  342.4 1.6 select_reduce_fusion
  352.4 87.5 %reduce-scatter.8.cloned.1.call-done = f32[16,256]{1,0:T(8,128)} async-done(((f32[256,256]{1,0:T(8,128)}), f32[16,256]{1,0:T(8,128)}) %reduce-scatter.8.cloned.1.call-update) | async-done | bytes 16400 | tf_op jit(solution)/shard_map/reduce_scatter | solution.py:120
  (136 shorter events, 46.3 us)
Async XLA Ops:
  8.0 78.1 %all-reduce.7.cloned.1.call-start = ((), (), s32[]{:S(2)}) async-start(), calls=%async_computation.5 | async-start | bytes 524288 | tf_op jit(solution)/shard_map/psum | solution.py:56
  52.3 41.1 %all-reduce.5.cloned.1.call-start = ((), (), s32[]{:S(2)}) async-start(), calls=%async_computation.4 | async-start | bytes 524288 | tf_op jit(solution)/shard_map/psum | solution.py:55
  71.1 45.6 %reduce-scatter.4.cloned.1.call-start = ((), (), s32[]{:S(2)}) async-start(), calls=%async_computation.3 | async-start | bytes 327680 | tf_op jit(solution)/shard_map/reduce_scatter | solution.py:79
  71.2 45.6 %copy-start.8 = (bf16[1,64,256]{2,1,0:T(8,128)(2,1)S(1)}, bf16[1,64,256]{2,1,0:T(8,128)(2,1)}, u32[]{:S(2)}) copy-start(bf16[1,64,256]{2,1,0:T(8,128)(2,1)} %param.15) | copy-start | bytes 98308
  85.3 0.7 copy-start.2
  86.0 112.7 %all-reduce.9.cloned.1.call-start = ((), (), s32[]{:S(2)}) async-start(), calls=%async_computation.7 | async-start | bytes 524288 | tf_op jit(solution)/shard_map/psum | solution.py:83
  121.2 6.4 %copy-start.5 = (bf16[64,256]{1,0:T(8,128)(2,1)}, bf16[64,256]{1,0:T(8,128)(2,1)S(1)}, u32[]{:S(2)}) copy-start(bf16[64,256]{1,0:T(8,128)(2,1)S(1)} %fusion.15) | copy-start | bytes 98308
  127.6 11.1 %copy-start.10 = (s32[2,3]{1,0:T(2,128)S(1)}, s32[2,3]{1,0:T(2,128)}, u32[]{:S(2)}) copy-start(s32[2,3]{1,0:T(2,128)} %get-tuple-element.488) | copy-start | bytes 76
  127.6 165.4 %reduce-scatter.6.cloned.1.call-start = ((), (), s32[]{:S(2)}) async-start(), calls=%async_computation.6 | async-start | bytes 278528 | tf_op jit(solution)/shard_map/reduce_scatter | solution.py:104
  138.7 60.0 %copy-start.3 = (f32[256,256]{1,0:T(8,128)S(1)}, f32[256,256]{1,0:T(8,128)}, u32[]{:S(2)}) copy-start(f32[256,256]{1,0:T(8,128)} %all-reduce.7.cloned.1.call-done) | copy-start | bytes 786436
  138.7 154.3 %copy-start.6 = (bf16[1,16,256]{2,1,0:T(8,128)(2,1)S(1)}, bf16[1,16,256]{2,1,0:T(8,128)(2,1)}, u32[]{:S(2)}) copy-start(bf16[1,16,256]{2,1,0:T(8,128)(2,1)} %param.16) | copy-start | bytes 24580
  188.2 0.7 copy-start
  189.0 153.5 %all-reduce.11.cloned.1.call-start = ((), (), s32[]{:S(2)}) async-start(), calls=%async_computation.9 | async-start | bytes 524288 | tf_op jit(solution)/shard_map/psum | solution.py:108
  296.8 20.8 %copy-start.9 = (bf16[16,256]{1,0:T(8,128)(2,1)}, bf16[16,256]{1,0:T(8,128)(2,1)S(1)}, u32[]{:S(2)}) copy-start(bf16[16,256]{1,0:T(8,128)(2,1)S(1)} %fusion.18) | copy-start | bytes 24580
  317.5 122.4 %reduce-scatter.8.cloned.1.call-start = ((), (), s32[]{:S(2)}) async-start(), calls=%async_computation.8 | async-start | bytes 278528 | tf_op jit(solution)/shard_map/reduce_scatter | solution.py:120
  317.6 24.9 %copy-start.4 = (f32[256,256]{1,0:T(8,128)S(1)}, f32[256,256]{1,0:T(8,128)}, u32[]{:S(2)}) copy-start(f32[256,256]{1,0:T(8,128)} %all-reduce.9.cloned.1.call-done) | copy-start | bytes 786436
  317.6 122.3 %copy-start.7 = (bf16[1,16,256]{2,1,0:T(8,128)(2,1)S(1)}, bf16[1,16,256]{2,1,0:T(8,128)(2,1)}, u32[]{:S(2)}) copy-start(bf16[1,16,256]{2,1,0:T(8,128)(2,1)} %param.17) | copy-start | bytes 24580
  341.7 0.7 copy-start.1
Sparse Core Ops, SparseCore 0:
  52.4 14.0 all-reduce.6
  71.2 22.1 all-reduce.4
  127.7 70.9 all-reduce.8
  317.6 20.5 all-reduce.10
Sparse Core Ops, SparseCore 1:
  86.1 30.6 reduce-scatter.3
  189.0 103.9 reduce-scatter.5
  342.5 97.3 reduce-scatter.7
where the time goes:
time: 454 us; the launch traced here: 452 us
  waiting for transfers between devices  202 us (44%)
  blocking collectives  86.3 us (19%)
  matrix products  54.4 us (12%)
  local copies, waits for them, and re-layouts  45.9 us (10%)
  other arithmetic  22.2 us (5%)
  loops' own time  20.3 us (4%)
  between operations  20.1 us (4%)
    reduce_scatter x1, waiting for transfers between devices, on_device(): lax.psum_scatter(partial_c, ('gx', 'gy'), scatter_dimension=0, tiled=True)  87.5 us
    reduce_scatter x1, waiting for transfers between devices, on_device(): lax.psum_scatter(partial_b, ('gx', 'gz'), scatter_dimension=0, tiled=True)  84.3 us
    all_gather x1, blocking collectives, on_device(): slab_c = lax.all_gather(own_c, ('gx', 'gy'), axis=0, tiled=True)  43.3 us
    while x3, local copies, waits for them, and re-layouts  24.6 us
    all_gather x1, blocking collectives, on_device(): slab_b_new = lax.all_gather(new_b, ('gx', 'gz'), axis=0, tiled=True)  19.8 us
    all_gather x1, blocking collectives, on_device(): slab_b = lax.all_gather(own_b, ('gx', 'gz'), axis=0, tiled=True)  17.8 us
    dot_general x1, matrix products, second_visit(): lax.dot_general(band_a, block.reshape(side, side * side), (((0,), (0,)),...  15 us
    reduce_scatter x1, waiting for transfers between devices, on_device(): lax.psum_scatter(partial_a, ('gy', 'gz'), scatter_dimension=0, tiled=True)  13.3 us
  transfers between devices with their start and end apart: 7, of which 5 were waited for; matrix products, arithmetic and copies ran while one was open for 23% of the time, Pallas kernels for 0%

commit v1 on v0

--- a/solution.py
+++ b/solution.py
@@ -6,6 +6,24 @@
 NS_STEPS = 8
 ADMM_ITERS = 4
 HIGHEST = lax.Precision.HIGHEST
+
+
+def in_order(blocks, dim):
+    shape = list(blocks.shape[1:])
+    shape[dim] *= blocks.shape[0]
+    return jnp.moveaxis(blocks, 0, dim).reshape(shape)
+
+
+def doubled(value, axis):
+    length = lax.axis_size(axis)
+    parts = value[None]
+    for level in range(length.bit_length() - 1):
+        bit = 1 << level
+        other = lax.ppermute(parts, axis, [(i, i ^ bit) for i in range(length)])
+        both = jnp.stack([parts, other])
+        upper = lax.axis_index(axis) >> level & 1
+        parts = jnp.where(upper == 0, both, both[::-1]).reshape(-1, *value.shape)
+    return parts
 
 
 def gram_rows(factor):
@@ -50,7 +68,7 @@
     own_b = factor_b[0]
     own_c = factor_c[0]
     slab_b = lax.all_gather(own_b, ("gx", "gz"), axis=0, tiled=True)
-    slab_c = lax.all_gather(own_c, ("gx", "gy"), axis=0, tiled=True)
+    slab_c = in_order(doubled(own_c, ("gx", "gy")), 0)
     height = slab_b.shape[0]
     gram_b = lax.psum(gram_rows(slab_b), "gy")
     gram_c = lax.psum(gram_rows(slab_c), "gz")

time: 454 us -> 433 us (0.954)
  blocking collectives: 86.3 us -> 46.3 us
  waiting for transfers between devices: 202 us -> 214 us
  starting transfers between devices: 0.51 us -> 7.87 us
    all_gather x1 -> x0, blocking collectives: 43.3 us -> none  [on_device(): slab_c = lax.all_gather(own_c, ('gx', 'gy'), axis=0, tiled=True)]
    psum x1, waiting for transfers between devices: 0.02 us -> 20.6 us  [on_device(): gram_c = lax.psum(gram_rows(slab_c), 'gz')]
    reduce_scatter x1, waiting for transfers between devices: 13.3 us -> 0.03 us  [on_device(): lax.psum_scatter(partial_a, ('gy', 'gz'), scatter_dimension=0, tiled=True)]
    ppermute x0 -> x4, waiting for transfers between devices: none -> 7.78 us  [doubled(): other = lax.ppermute(parts, axis, [(i, i ^ bit) for i in range(length)])]
    ppermute x0 -> x4, starting transfers between devices: none -> 7.36 us  [doubled(): other = lax.ppermute(parts, axis, [(i, i ^ bit) for i in range(length)])]
  transfers between devices with their start and end apart: 7 -> 11, of which waited for: 5 -> 8; matrix products, arithmetic and copies ran while one was open for 23% -> 25% of each run, Pallas kernels for 0% -> 0%
where the time goes in v1:
time: 433 us; the launch traced here: 432 us
  waiting for transfers between devices  214 us (49%)
  matrix products  54.4 us (13%)
  blocking collectives  46.3 us (11%)
  local copies, waits for them, and re-layouts  45.9 us (11%)
  other arithmetic  23 us (5%)
  loops' own time  20.2 us (5%)
  between operations  20.2 us (5%)
  starting transfers between devices  7.87 us (2%)
    reduce_scatter x1, waiting for transfers between devices, on_device(): lax.psum_scatter(partial_c, ('gx', 'gy'), scatter_dimension=0, tiled=True)  87.5 us
    reduce_scatter x1, waiting for transfers between devices, on_device(): lax.psum_scatter(partial_b, ('gx', 'gz'), scatter_dimension=0, tiled=True)  84.1 us
    while x3, local copies, waits for them, and re-layouts  24.6 us
    all_gather x1, blocking collectives, on_device(): slab_b = lax.all_gather(own_b, ('gx', 'gz'), axis=0, tiled=True)  21.1 us
    psum x1, waiting for transfers between devices, on_device(): gram_c = lax.psum(gram_rows(slab_c), 'gz')  20.6 us
    all_gather x1, blocking collectives, on_device(): slab_b_new = lax.all_gather(new_b, ('gx', 'gz'), axis=0, tiled=True)  19.8 us
    dot_general x1, matrix products, second_visit(): lax.dot_general(band_a, block.reshape(side, side * side), (((0,), (0,)),...  15 us
    dot_general x12, matrix products, split_updates(): jnp.dot(totals + penalty * (primal + dual), inverse, precision=HIGHEST)  12.6 us
  transfers between devices with their start and end apart: 11, of which 8 were waited for; matrix products, arithmetic and copies ran while one was open for 25% of the time, Pallas kernels for 0%

profile of v1, /device:TPU:0, one launch (start us, length us, event | category | flops | bytes accessed | tf_op | source)
XLA Modules:
  0.0 431.6 jit_solution(9585368864245833262)
XLA Ops:
  8.0 3.0 collective-permute-start
  13.6 2.1 collective-permute-start.1
  17.5 2.1 collective-permute-start.2
  19.6 21.1 %all-gather = bf16[1,256,256]{2,1,0:T(8,128)(2,1)S(1)} all-gather(bf16[1,16,256]{2,1,0:T(8,128)(2,1)} %param.16), channel_id=2, replica_groups=mesh['gx'=8,'gy'=2,'gz'=2] {'gx','gz'}, dimensions={1}, use_global_device_ids=true | all-gather | bytes 139264 | tf_op jit(solution)/shard_map/all_gather | solution.py:70
  41.8 4.2 collective-permute-done.3
  47.2 14.0 %while.32 = (s32[]{:T(128)}, f32[256,256]{1,0:T(8,128)S(1)}, s32[]{:T(128)}, s32[2,3]{1,0:T(2,128)}, bf16[2,128,128,128]{3,2,1,0:T(8,128)(2,1)}, /*index=5*/bf16...) while((s32[]{:T(128)}, f32[256,256]{1,0:T(8,128)S(1)}, ...), condition=%wide.region_2.3_spmd, body=%wide.region_0.2_spmd.sunk | while | flops 1082163200 | bytes 5374269 | solution.py:96
  53.0 4.5 %multiply_reduce_fusion.4 = f32[128,256]{1,0:T(8,128)S(1)} fusion(f32[128,256]{1,0:T(8,128)S(1)} %dynamic-slice_convert_fusion.2, bf16[2,128,128,128]{3,2,1,0:T(8,128)(2,1)} %get-tuple-element.401, s32[]{:T(128)S(6)} %select_n.128, bf16[256,256]{1,0:T(8,128)(2,1)S(1)} %get-tuple-element.402, s32[]{:T(128)S(6)} %select_n.130), kind=kOutput, calls=%fused_computation.clone.1 | convolution fusion | flops 1082097664 | bytes 4521992 | tf_op jit(solution)/shard_map/while/body/dot_general | solution.py:89
  61.9 2.9 all-reduce.5.cloned.1.call-done
  64.8 20.6 %all-reduce.7.cloned.1.call-done = f32[256,256]{1,0:T(8,128)} async-done(((f32[256,256]{1,0:T(8,128)}), f32[256,256]{1,0:T(8,128)}) %all-reduce.7.cloned.1.call-update) | async-done | bytes 262160 | tf_op jit(solution)/shard_map/psum | solution.py:74
  100.0 5.4 %all_gather.10 = bf16[256,256]{1,0:T(8,128)(2,1)S(1)} all-gather(bf16[64,256]{1,0:T(8,128)(2,1)S(1)} %fusion.15), channel_id=1, replica_groups=mesh['gx'=8,'gy'=2,'gz'=2] {'gy','gz'}, dimensions={0}, use_global_device_ids=true | all-gather | bytes 163840 | tf_op jit(solution)/shard_map/all_gather | solution.py:100
  106.4 11.0 %broadcast_in_dim.28 = f32[2,256,16384]{2,1,0:T(8,128)} broadcast(f32[]{:T(128)} %constant.96.clone.1), dimensions={} | broadcast | bytes 33554436 | tf_op jit(solution)/shard_map/broadcast_in_dim | solution.py:120
  117.5 49.5 %while.33 = (s32[]{:T(128)}, f32[256,256]{1,0:T(8,128)S(1)}, f32[2,256,16384]{2,1,0:T(8,128)}, s32[]{:T(128)}, s32[2,3]{1,0:T(2,128)S(1)}, /*index=5*/bf16[256,2...) while((s32[]{:T(128)}, f32[256,256]{1,0:T(8,128)S(1)}, ...), condition=%wide.region_11.12_spmd, body=%wide.region_9.11_spmd.sunk | while | flops 1082163200 | bytes 98697544 | solution.py:121
  121.1 2.5 constant_dynamic-slice_fusion.14
  123.6 15.0 %bitcast_dynamic-update-slice_fusion.2 = (f32[2,256,16384]{2,1,0:T(8,128)}, f32[256,16384]{1,0:T(8,128)}) fusion(f32[2,256,16384]{2,1,0:T(8,128)} %get-tuple-element.422, s32[]{:T(128)S(6)} %select_n.132, bf16[16,8,128,128]{3,2,1,0:T(8,128)(2,1)S(1)} %bitcast.205, bf16[256,256]{1,0:T(8,128)(2,1)S(1)} %get-tuple-element.437, s32[]{:T(128)S(6)} %select_n.134), kind=kOutput, calls=%fused_computation.10.clone.1 | convolution fusion | flops 1073741824 | bytes 37814280 | tf_op jit(solution)/shard_map/while/body/dot_general | solution.py:108
  138.6 14.1 %copy.55 = f32[32,8,128,128]{3,2,1,0:T(8,128)} copy(f32[32,8,128,128]{3,1,2,0:T(8,128)} %bitcast.204) | data formatting | bytes 33554432 | tf_op jit(solution)/shard_map/while
  154.8 8.2 %multiply_reduce_fusion.5 = f32[256,128]{1,0:T(8,128)S(1)} fusion(f32[256,128,128]{2,1,0:T(8,128)} %bitcast.203, f32[256,128]{1,0:T(8,128)S(1)} %convert_bitcast_fusion.4), kind=kLoop, calls=%fused_computation.11.clone.1 | loop fusion | flops 8355840 | bytes 17039360 | tf_op jit(solution)/shard_map/while/body/reduce_sum | solution.py:114
  168.0 10.8 %all-reduce.9.cloned.1.call-done = f32[256,256]{1,0:T(8,128)} async-done(((f32[256,256]{1,0:T(8,128)}), f32[256,256]{1,0:T(8,128)}) %all-reduce.9.cloned.1.call-update) | async-done | bytes 262160 | tf_op jit(solution)/shard_map/psum | solution.py:101
  188.8 84.1 %reduce-scatter.6.cloned.1.call-done = f32[16,256]{1,0:T(8,128)} async-done(((f32[256,256]{1,0:T(8,128)}), f32[16,256]{1,0:T(8,128)}) %reduce-scatter.6.cloned.1.call-update) | async-done | bytes 16400 | tf_op jit(solution)/shard_map/reduce_scatter | solution.py:122
  276.7 19.8 %all_gather.11 = bf16[256,256]{1,0:T(8,128)(2,1)S(1)} all-gather(bf16[16,256]{1,0:T(8,128)(2,1)S(1)} %fusion.18), channel_id=1, replica_groups=mesh['gx'=8,'gy'=2,'gz'=2] {'gx','gz'}, dimensions={0}, use_global_device_ids=true | all-gather | bytes 139264 | tf_op jit(solution)/shard_map/all_gather | solution.py:125
  297.6 24.1 %while.34 = (s32[]{:T(128)}, f32[256,256]{1,0:T(8,128)S(1)}, s32[]{:T(128)}, s32[2,3]{1,0:T(2,128)S(1)}, f32[2,256,16384]{2,1,0:T(8,128)}, /*index=5*/bf16[256,2...) while((s32[]{:T(128)}, f32[256,256]{1,0:T(8,128)S(1)}, s32[]{:T(128)}, ...), condition=%wide.region_19.20_spmd, body=%wide.region_17.19_spmd.sunk | while | flops 8421390 | bytes 86049016 | solution.py:137
  301.0 6.6 %dynamic-slice_bitcast_fusion.2 = f32[32,8,128,128]{3,1,2,0:T(8,128)S(1)} fusion(f32[2,256,16384]{2,1,0:T(8,128)} %get-tuple-element.468, s32[]{:T(128)S(6)} %select_n.136), kind=kLoop, calls=%fused_computation.26.clone.1 | loop fusion | bytes 33554436 | tf_op jit(solution)/shard_map/while
  307.7 3.8 copy.59
  311.5 6.1 %fusion.284 = f32[256,128]{1,0:T(8,128)S(1)} fusion(f32[32,8,128,128]{3,2,1,0:T(8,128)S(1)} %copy.59, f32[256,128]{1,0:T(8,128)S(1)} %convert_bitcast_fusion.5), kind=kLoop, calls=%fused_computation.25.clone.1 | loop fusion | flops 8355840 | bytes 17039360 | tf_op jit(solution)/shard_map/while/body/reduce_sum | solution.py:132
  332.4 87.5 %reduce-scatter.8.cloned.1.call-done = f32[16,256]{1,0:T(8,128)} async-done(((f32[256,256]{1,0:T(8,128)}), f32[16,256]{1,0:T(8,128)}) %reduce-scatter.8.cloned.1.call-update) | async-done | bytes 16400 | tf_op jit(solution)/shard_map/reduce_scatter | solution.py:138
  (151 shorter events, 55.6 us)
Async XLA Ops:
  8.0 56.8 %all-reduce.5.cloned.1.call-start = ((), (), s32[]{:S(2)}) async-start(), calls=%async_computation.4 | async-start | bytes 524288 | tf_op jit(solution)/shard_map/psum | solution.py:73
  8.0 4.9 %collective-permute-start = (bf16[1,16,256]{2,1,0:T(8,128)(2,1)}, bf16[1,16,256]{2,1,0:T(8,128)(2,1)S(1)}, u32[]{:S(2)}, u32[]{:S(2)}) collective-permute-start(bf16[1,16,256]{2,1,0:T(8,128)(2,1)} %param.17), channel_id=1, source_target_pairs={{0,2},{2,0},{4,6},{6,4},{8,10},{10,8},{12,14},{14,12},{16,18},{18,... | collective-permute-start | bytes 24584 | tf_op jit(solution)/shard_map/ppermute | solution.py:22
  13.6 3.8 collective-permute-start.1
  17.5 23.2 %collective-permute-start.2 = (bf16[4,16,256]{2,1,0:T(8,128)(2,1)S(1)}, bf16[4,16,256]{2,1,0:T(8,128)(2,1)S(1)}, u32[]{:S(2)}, u32[]{:S(2)}) collective-permute-start(bf16[4,16,256]{2,1,0:T(8,128)(2,1)S(1)} %bitcast.211), channel_id=1, source_target_pairs={{0,8},{2,10},{4,12},{6,14},{8,0},{10,2},{12,4},{14,6},{16,24},{18,... | collective-permute-start | bytes 98312 | tf_op jit(solution)/shard_map/ppermute | solution.py:22
  40.8 5.3 %collective-permute-start.3 = (bf16[8,16,256]{2,1,0:T(8,128)(2,1)S(1)}, bf16[8,16,256]{2,1,0:T(8,128)(2,1)S(1)}, u32[]{:S(2)}, u32[]{:S(2)}) collective-permute-start(bf16[8,16,256]{2,1,0:T(8,128)(2,1)S(1)} %bitcast.209), channel_id=1, source_target_pairs={{0,16},{2,18},{4,20},{6,22},{8,24},{10,26},{12,28},{14,30},{16,0},... | collective-permute-start | bytes 196616 | tf_op jit(solution)/shard_map/ppermute | solution.py:22
  41.8 43.6 %all-reduce.7.cloned.1.call-start = ((), (), s32[]{:S(2)}) async-start(), calls=%async_computation.5 | async-start | bytes 524288 | tf_op jit(solution)/shard_map/psum | solution.py:74
  47.1 48.4 %reduce-scatter.4.cloned.1.call-start = ((), (), s32[]{:S(2)}) async-start(), calls=%async_computation.3 | async-start | bytes 327680 | tf_op jit(solution)/shard_map/reduce_scatter | solution.py:97
  47.1 48.4 %copy-start.8 = (bf16[1,64,256]{2,1,0:T(8,128)(2,1)S(1)}, bf16[1,64,256]{2,1,0:T(8,128)(2,1)}, u32[]{:S(2)}) copy-start(bf16[1,64,256]{2,1,0:T(8,128)(2,1)} %param.15) | copy-start | bytes 98308
  61.1 0.7 copy-start.2
  61.9 116.9 %all-reduce.9.cloned.1.call-start = ((), (), s32[]{:S(2)}) async-start(), calls=%async_computation.7 | async-start | bytes 524288 | tf_op jit(solution)/shard_map/psum | solution.py:101
  99.9 6.5 %copy-start.5 = (bf16[64,256]{1,0:T(8,128)(2,1)}, bf16[64,256]{1,0:T(8,128)(2,1)S(1)}, u32[]{:S(2)}) copy-start(bf16[64,256]{1,0:T(8,128)(2,1)S(1)} %fusion.15) | copy-start | bytes 98308
  106.3 11.1 %copy-start.10 = (s32[2,3]{1,0:T(2,128)S(1)}, s32[2,3]{1,0:T(2,128)}, u32[]{:S(2)}) copy-start(s32[2,3]{1,0:T(2,128)} %get-tuple-element.512) | copy-start | bytes 76
  106.3 166.6 %reduce-scatter.6.cloned.1.call-start = ((), (), s32[]{:S(2)}) async-start(), calls=%async_computation.6 | async-start | bytes 278528 | tf_op jit(solution)/shard_map/reduce_scatter | solution.py:122
  117.4 61.3 %copy-start.4 = (f32[256,256]{1,0:T(8,128)S(1)}, f32[256,256]{1,0:T(8,128)}, u32[]{:S(2)}) copy-start(f32[256,256]{1,0:T(8,128)} %all-reduce.7.cloned.1.call-done) | copy-start | bytes 786436
  117.4 155.5 %copy-start.6 = (bf16[1,16,256]{2,1,0:T(8,128)(2,1)S(1)}, bf16[1,16,256]{2,1,0:T(8,128)(2,1)}, u32[]{:S(2)}) copy-start(bf16[1,16,256]{2,1,0:T(8,128)(2,1)} %param.16) | copy-start | bytes 24580
  167.0 0.7 copy-start
  167.7 154.7 %all-reduce.11.cloned.1.call-start = ((), (), s32[]{:S(2)}) async-start(), calls=%async_computation.9 | async-start | bytes 524288 | tf_op jit(solution)/shard_map/psum | solution.py:126
  276.7 20.8 %copy-start.9 = (bf16[16,256]{1,0:T(8,128)(2,1)}, bf16[16,256]{1,0:T(8,128)(2,1)S(1)}, u32[]{:S(2)}) copy-start(bf16[16,256]{1,0:T(8,128)(2,1)S(1)} %fusion.18) | copy-start | bytes 24580
  297.5 122.4 %reduce-scatter.8.cloned.1.call-start = ((), (), s32[]{:S(2)}) async-start(), calls=%async_computation.8 | async-start | bytes 278528 | tf_op jit(solution)/shard_map/reduce_scatter | solution.py:138
  297.5 24.9 %copy-start.3 = (f32[256,256]{1,0:T(8,128)S(1)}, f32[256,256]{1,0:T(8,128)}, u32[]{:S(2)}) copy-start(f32[256,256]{1,0:T(8,128)} %all-reduce.9.cloned.1.call-done) | copy-start | bytes 786436
  297.5 122.3 %copy-start.7 = (bf16[1,16,256]{2,1,0:T(8,128)(2,1)S(1)}, bf16[1,16,256]{2,1,0:T(8,128)(2,1)}, u32[]{:S(2)}) copy-start(bf16[1,16,256]{2,1,0:T(8,128)(2,1)} %param.17) | copy-start | bytes 24580
  321.7 0.7 copy-start.1
Sparse Core Ops, SparseCore 0:
  41.9 22.8 all-reduce.4
  67.1 18.2 all-reduce.6
  106.5 72.2 all-reduce.8
  297.6 20.5 all-reduce.10
Sparse Core Ops, SparseCore 1:
  62.0 30.1 reduce-scatter.3
  167.8 105.0 reduce-scatter.5
  322.5 97.3 reduce-scatter.7
